TPU v7x, 256 devices: a whole 4x4x8 slice. The times are simulated.
256 devices in a mesh: seq: 64 (over z_lo, x, y), tp: 4 (over z_hi, core).
Axes of the slice: x: 4, y: 4, z: 8 (z_hi: 2, z_lo: 4; z = z_hi * 4 + z_lo), core: 2. Of those that a mesh axis runs over, the one named last changes fastest.
Arguments:
- byte_states: bfloat16 [16384, 1024], P('seq'), may hold values from -6 to 6
- enc_gain: bfloat16 [1024], replicated, may hold values from 0.25 to 1.75
- enc_qkv: bfloat16 [3, 1024, 1024], P(None, None, 'tp')
- enc_proj_out: bfloat16 [1024, 1024], P('tp'), may hold values from -0.1875 to 0.1875
- starts: int32 [64, 64], P('seq'), may hold values from 0 to 16384, as said below
- counts: int32 [64], P('seq'), may hold values from 32 to 64, as said below
- lift: bfloat16 [1024, 4096], P(None, 'tp')
- cross_kv: bfloat16 [2, 1024, 4096], P(None, None, 'tp')
- latent_gain: bfloat16 [4096], replicated, may hold values from 0.25 to 1.75
- lat_qkv: bfloat16 [3, 4096, 2048], P(None, 'seq', 'tp')
- lat_proj_out: bfloat16 [2048, 4096], P('tp', 'seq'), may hold values from -0.75 to 0.75
Outputs:
- byte_out: bfloat16 [16384, 1024], P('seq')
- latent_out: bfloat16 [4096, 4096], P('seq', 'tp')
Inputs may be any that keep to these rules, and one draw needn't show every extreme that they name: `starts`: row s lists in increasing order the first byte (counted over all 16384 bytes) of each patch beginning in bytes s * 256 to (s + 1) * 256 - 1, then 16384 in unused places. Byte 0 begins a patch; every row's first patch begins fewer than 8 bytes into its block, and in some row exactly 7 bytes in. counts[s] is the number of patches listed in row s of starts; some row holds 64.
All inputs are finite; a program needn't handle non-finite values.
Results may differ from a plain program's by a relative error of at most 0.018.
Values may be sent and summed in bfloat16 or wider, within the bound.
No kernel may reach another device: no remote copies, remote signals or barrier semaphores. Data moves between devices by JAX's collectives and lax.ppermute only.
A program may use at most 128 MiB of HBM per device.

v0:
```python
import math

import jax
import jax.numpy as jnp
from jax import lax
from jax.sharding import Mesh
from jax.sharding import PartitionSpec as P

EH = 64
HD = 128
WIN = 512
SPILL = 8
SEQ = ("seq_0", "seq_1", "seq_2")


epsilon = 1e-05
rope_base = 500000.0
far_position = 1 << 30


def from_behind(value, axis, steps):
    count = lax.axis_size(axis)
    leading, last = (max(0, -steps), min(count, count - steps))
    return lax.ppermute(value, axis, [(source, source + steps) for source in range(leading, last)])


def from_everyone(value, axis):
    copies = jnp.broadcast_to(value, (lax.axis_size(axis), *value.shape))
    return lax.all_to_all(copies, axis, split_axis=0, concat_axis=0, tiled=True)


def taken_together(value, axis):
    everything = from_everyone(value, axis)
    return jnp.sum(everything, axis=0)


def combined_pairwise(pieces, combine):
    while len(jax.tree.leaves(pieces)[0]) > 1:
        pieces = jax.vmap(combine)(*(pieces[side::2] for side in (0, 1)))
    return pieces[0]


def carried_in(value, axis, combine, identity):
    length, index = (lax.axis_size(axis), lax.axis_index(axis))
    passed = jnp.arange(length) < index

    def kept(part, zero, own):
        part = jnp.where(
            passed.reshape(-1, *(1 for _ in own.shape)), part, jnp.asarray(zero, own.dtype)
        )
        return part

    pieces = from_everyone(value, axis)
    return combined_pairwise(kept(pieces, identity, value), combine)


def laid_out(tiles, dim):
    tiles = jnp.moveaxis(tiles, 0, dim)
    lengths = tiles.shape
    return tiles.reshape(*lengths[:dim], lengths[dim] * lengths[dim + 1], *lengths[dim + 2 :])


def gather_directly(value, axis, dim):
    tiles = from_everyone(value, axis)
    return laid_out(tiles, dim)


def edges_of(length, count):
    unit = 8 if length >= 8 * count else 1
    return [length // unit * k // count * unit for k in range(1, count)]


def gather_in_order(value, axes, turns):
    tiles = value
    for k in turns:
        tiles = lax.all_gather(tiles, axes[k])
    done = turns[::-1]
    back = [done.index(k) for k in range(len(axes))]
    tiles = tiles.transpose(*back, *range(len(axes), tiles.ndim))
    return tiles.reshape(-1, *value.shape)


def spread_gather(value, axes, dim):
    cut = max(range(max(1, value.ndim - 1)), key=lambda d: value.shape[d])
    count, done = (len(axes), [])
    for leading, slab in enumerate(jnp.split(value, edges_of(value.shape[cut], count), axis=cut)):
        if slab.size:
            turns = [(leading - k) % count for k in range(count)]
            done.append(gather_in_order(slab, axes, turns))
    return laid_out(jnp.concatenate(done, axis=cut + 1), dim)


def sent_together(arrays, axis, dim, along):
    ends, at = ([], 0)
    for a in arrays[:-1]:
        at += a.shape[along]
        ends.append(at)
    both = jnp.concatenate(arrays, axis=along)
    return tuple(jnp.split(lax.all_gather(both, axis, axis=dim, tiled=True), ends, axis=along))


def shortened(value):

    def short(part):
        return part.astype(jnp.bfloat16) if part.dtype == jnp.float32 else part

    return jax.tree.map(short, value)


def in_blocks(value, dim, length):
    before, after = (value.shape[:dim], value.shape[dim + 1 :])
    return jnp.moveaxis(value.reshape(*before, length, -1, *after), dim, 0)


def sum_at_owner(value, axis, dim):
    length = lax.axis_size(axis)
    tiles = lax.all_to_all(in_blocks(value, dim, length), axis, 0, 0, tiled=True)
    return jnp.sum(tiles, axis=0)


def rms_scale(values, gain_row):
    mean_square = jnp.mean(values * values, axis=-1, keepdims=True)
    return values * lax.rsqrt(mean_square + epsilon) * gain_row


def masked_softmax(scores, allowed):
    scores = jnp.where(allowed, scores, -1e30)
    largest = jnp.max(scores, axis=-1, keepdims=True)
    raised = jnp.where(allowed, jnp.exp(scores - largest), 0.0)
    return raised / jnp.sum(raised, axis=-1, keepdims=True)


def rotate(values, position):
    halfway = values.shape[-1] // 2
    frequency = jnp.power(
        rope_base, -2.0 * jnp.arange(halfway, dtype=jnp.float32) / values.shape[-1]
    )
    angles = position.astype(jnp.float32)[:, None] * frequency[None, :]
    cosine = jnp.cos(angles)[:, None, :]
    sine_rows = jnp.sin(angles)[:, None, :]
    lower_half = values[..., :halfway]
    upper_half = values[..., halfway:]
    return jnp.concatenate(
        [
            lower_half * cosine - upper_half * sine_rows,
            upper_half * cosine + lower_half * sine_rows,
        ],
        axis=-1,
    )


def patch_block(extended, first_byte, end_byte, in_use, anchor, lift, cross_kv):
    columns = anchor + jnp.arange(extended.shape[0], dtype=jnp.int32)
    inside = (
        (columns[None, :] >= first_byte[:, None])
        & (columns[None, :] < end_byte[:, None])
        & in_use[:, None]
    )
    member = inside.astype(jnp.bfloat16)
    totals = jnp.dot(member, extended, preferred_element_type=jnp.float32)
    lengths = jnp.maximum(jnp.sum(inside.astype(jnp.float32), axis=1), 1.0)
    pooled = (totals / lengths[:, None]).astype(jnp.bfloat16)
    lifted = jnp.dot(pooled, lift, preferred_element_type=jnp.float32)
    key_rows = jnp.dot(extended, cross_kv[0], preferred_element_type=jnp.float32).astype(
        jnp.bfloat16
    )
    value_rows = jnp.dot(extended, cross_kv[1], preferred_element_type=jnp.float32).astype(
        jnp.bfloat16
    )
    slot_total = first_byte.shape[0]
    head_count = lifted.shape[1] // HD
    queries = lifted.astype(jnp.bfloat16).reshape(slot_total, head_count, HD)
    scores = jnp.einsum(
        "phd,khd->hpk",
        queries,
        key_rows.reshape(-1, head_count, HD),
        preferred_element_type=jnp.float32,
    ) * (1.0 / math.sqrt(HD))
    allowed = inside | (~in_use)[:, None] & (columns[None, :] == anchor)
    weights = masked_softmax(scores, allowed[None]).astype(jnp.bfloat16)
    crossed = jnp.einsum(
        "hpk,khd->phd",
        weights,
        value_rows.reshape(-1, head_count, HD),
        preferred_element_type=jnp.float32,
    )
    crossed = crossed.reshape(slot_total, head_count * HD)
    return jnp.where(in_use[:, None], lifted + crossed, 0.0).astype(jnp.bfloat16)


def add_counts(earlier, later):
    return earlier + later


def shards(
    byte_states,
    enc_gain,
    enc_qkv,
    enc_proj_out,
    starts,
    counts,
    lift,
    cross_kv,
    latent_gain,
    lat_qkv,
    lat_proj_out,
):
    byte_rows = byte_states.shape[0]
    anchor = lax.axis_index(SEQ) * byte_rows
    states = byte_states.astype(jnp.float32)
    normed = rms_scale(states, enc_gain.astype(jnp.float32)).astype(jnp.bfloat16)
    projected = jnp.einsum(
        "bd,idc->ibc", normed, enc_qkv, preferred_element_type=jnp.float32
    ).astype(jnp.bfloat16)
    reach_blocks = max(WIN // byte_rows, 1)
    tail_rows = min(WIN, byte_rows)
    key_parts = []
    value_parts = []
    for distance in range(reach_blocks, 0, -1):
        moved_keys, moved_values = from_behind(
            (projected[1, byte_rows - tail_rows :], projected[2, byte_rows - tail_rows :]),
            SEQ,
            distance,
        )
        key_parts.append(moved_keys)
        value_parts.append(moved_values)
    key_rows = jnp.concatenate(key_parts + [projected[1]], axis=0)
    value_rows = jnp.concatenate(value_parts + [projected[2]], axis=0)
    head_count = projected.shape[2] // EH
    scores = jnp.einsum(
        "qhd,khd->hqk",
        projected[0].reshape(byte_rows, head_count, EH),
        key_rows.reshape(-1, head_count, EH),
        preferred_element_type=jnp.float32,
    ) * (1.0 / math.sqrt(EH))
    query_pos = anchor + jnp.arange(byte_rows, dtype=jnp.int32)
    key_pos = anchor - WIN + jnp.arange(WIN + byte_rows, dtype=jnp.int32)
    allowed = (
        (key_pos[None, :] <= query_pos[:, None])
        & (key_pos[None, :] > query_pos[:, None] - WIN)
        & (key_pos[None, :] >= 0)
    )
    weights = masked_softmax(scores, allowed[None]).astype(jnp.bfloat16)
    attended = jnp.einsum(
        "hqk,khd->qhd",
        weights,
        value_rows.reshape(-1, head_count, EH),
        preferred_element_type=jnp.float32,
    )
    attended = attended.reshape(byte_rows, head_count * EH).astype(jnp.bfloat16)
    blended = taken_together(
        jnp.dot(attended, enc_proj_out, preferred_element_type=jnp.float32), "tp"
    )
    encoded = (states + blended).astype(jnp.bfloat16)
    patch_count = counts[0]
    local_starts = starts[0]
    first_local = (local_starts[0:1] - anchor).astype(jnp.bfloat16)
    next_rows, next_first = from_behind((encoded[:SPILL], first_local), SEQ, -1)
    next_first = next_first.astype(jnp.int32)[0]
    extended = jnp.concatenate([encoded, next_rows], axis=0)
    slot_ids = jnp.arange(local_starts.shape[0], dtype=jnp.int32)
    in_use = slot_ids < patch_count
    following = jnp.concatenate([local_starts[1:], jnp.zeros((1,), jnp.int32)])
    patch_end = jnp.where(slot_ids + 1 < patch_count, following, anchor + byte_rows + next_first)
    patches = patch_block(extended, local_starts, patch_end, in_use, anchor, lift, cross_kv)
    offset = carried_in(counts, SEQ, add_counts, jnp.zeros((1,), jnp.int32))[0]
    position = offset + slot_ids
    slot_total = patches.shape[0]
    full_rows = gather_directly(patches, "tp", 1)
    normed_rows = rms_scale(full_rows.astype(jnp.float32), latent_gain.astype(jnp.float32)).astype(
        jnp.bfloat16
    )
    inner_width = lat_qkv.shape[2]
    projected = jnp.einsum(
        "pd,idc->ipc",
        normed_rows,
        spread_gather(lat_qkv, SEQ, 1),
        preferred_element_type=jnp.float32,
    )
    heads_here = inner_width // HD
    queries = rotate(projected[0].reshape(slot_total, heads_here, HD), position).astype(
        jnp.bfloat16
    )
    latent_keys = (
        rotate(projected[1].reshape(slot_total, heads_here, HD), position)
        .astype(jnp.bfloat16)
        .reshape(slot_total, inner_width)
    )
    latent_values = projected[2].astype(jnp.bfloat16)
    latent_pos = jnp.where(in_use, position, far_position)
    largest = jnp.full((heads_here, slot_total), -1e30, jnp.float32)
    piece_keys, piece_values, piece_pos = (
        *sent_together((latent_keys, latent_values), SEQ, 0, 1),
        lax.all_gather(shortened(latent_pos), SEQ, axis=0, tiled=True).astype(latent_pos.dtype),
    )
    rows_here = piece_keys.shape[0]
    piece_scores = jnp.einsum(
        "qhd,khd->hqk",
        queries,
        piece_keys.reshape(rows_here, heads_here, HD),
        preferred_element_type=jnp.float32,
    ) * (1.0 / math.sqrt(HD))
    permitted = (piece_pos[None, :] <= position[:, None])[None]
    piece_scores = jnp.where(permitted, piece_scores, -1e30)
    renewed = jnp.maximum(largest, jnp.max(piece_scores, axis=-1))
    raised = jnp.where(permitted, jnp.exp(piece_scores - renewed[..., None]), 0.0)
    weight_sum = jnp.sum(raised, axis=-1)
    weighted = jnp.einsum(
        "hqk,khd->hqd",
        raised.astype(jnp.bfloat16),
        piece_values.reshape(rows_here, heads_here, HD),
        preferred_element_type=jnp.float32,
    )
    largest, weight_sum, weighted = (renewed, weight_sum, weighted)
    latent_heads = (
        (weighted / weight_sum[..., None])
        .transpose(1, 0, 2)
        .reshape(slot_total, inner_width)
        .astype(jnp.bfloat16)
    )
    partials = jnp.dot(
        latent_heads,
        lax.all_gather(lat_proj_out, SEQ, axis=1, tiled=True),
        preferred_element_type=jnp.float32,
    )
    reduced = sum_at_owner(partials, "tp", 1)
    latent = jnp.where(in_use[:, None], patches.astype(jnp.float32) + reduced, 0.0).astype(
        jnp.bfloat16
    )
    return (encoded, latent)


def solution(mesh):
    finer = Mesh(mesh.devices.reshape(4, 4, 4, mesh.shape["tp"]), ("seq_0", "seq_1", "seq_2", "tp"))
    in_specs = (
        P(SEQ, None),
        P(),
        P(None, None, "tp"),
        P("tp", None),
        P(SEQ, None),
        P(SEQ),
        P(None, "tp"),
        P(None, None, "tp"),
        P(),
        P(None, SEQ, "tp"),
        P("tp", SEQ),
    )
    out_specs = (P(SEQ, None), P(SEQ, "tp"))
    return jax.shard_map(
        shards, mesh=finer, in_specs=in_specs, out_specs=out_specs, check_vma=False
    )
```

profile of v0, /device:TPU:1, one launch (start us, length us, event | category | flops | bytes accessed | tf_op | source)
XLA Modules:
  0.0 1065.7 jit_solution(14300211120696718170)
XLA Ops:
  8.3 11.9 %all-gather.3 = bf16[12,24,512]{2,1,0:T(8,128)(2,1)} all-gather(bf16[3,24,512]{2,1,0:T(8,128)(2,1)S(1)} %get-tuple-element.15), channel_id=5, replica_groups=mesh['seq_0'=4,'seq_1'=4,'seq_2'=4,'tp'=4] {'seq_1'}, dimensions={0}, use_global_device_ids=true | all-gather | bytes 368640 | tf_op jit(solution)/shard_map/all_gather | solution.py:76
  20.4 10.7 %all-gather.6 = bf16[12,24,512]{2,1,0:T(8,128)(2,1)} all-gather(bf16[3,24,512]{2,1,0:T(8,128)(2,1)S(1)} %get-tuple-element.16), channel_id=8, replica_groups=mesh['seq_0'=4,'seq_1'=4,'seq_2'=4,'tp'=4] {'seq_2'}, dimensions={0}, use_global_device_ids=true | all-gather | bytes 368640 | tf_op jit(solution)/shard_map/all_gather | solution.py:76
  31.9 13.9 %all-gather = bf16[12,16,512]{2,1,0:T(8,128)(2,1)S(1)} all-gather(bf16[3,16,512]{2,1,0:T(8,128)(2,1)S(1)} %split.15), channel_id=2, replica_groups=mesh['seq_0'=4,'seq_1'=4,'seq_2'=4,'tp'=4] {'seq_0'}, dimensions={0}, use_global_device_ids=true | all-gather | bytes 245760 | tf_op jit(solution)/shard_map/all_gather | solution.py:76
  45.8 12.3 %all-gather.1 = bf16[16,3,16,512]{3,2,1,0:T(8,128)(2,1)} all-gather(bf16[4,3,16,512]{3,2,1,0:T(8,128)(2,1)S(1)} %bitcast.170), channel_id=3, replica_groups=mesh['seq_0'=4,'seq_1'=4,'seq_2'=4,'tp'=4] {'seq_2'}, dimensions={0}, use_global_device_ids=true | all-gather | bytes 983040 | tf_op jit(solution)/shard_map/all_gather | solution.py:76
  58.2 5.4 all-gather.23.cloned.1.call-done
  63.9 2.2 fusion.41
  66.1 3.5 collective-permute-start.2
  69.6 3.2 collective-permute-start.3
  72.8 4.2 collective-permute-start
  77.0 2.5 collective-permute-start.1
  83.7 2.5 broadcast_in_dim.134
  86.2 13.0 %all-to-all-start = ((f32[4,256,1024]{2,1,0:T(8,128)}), f32[4,256,1024]{2,1,0:T(8,128)}, u32[]{:S(2)}, u32[]{:S(2)}) async-start(f32[4,256,1024]{2,1,0:T(8,128)} %broadcast_in_dim.134), calls=%async_computation | async-start | bytes 8388608 | tf_op jit(solution)/shard_map/all_to_all | solution.py:29
  101.9 2.7 collective-permute-done.4
  105.6 45.2 %all-to-all-done = f32[4,256,1024]{2,1,0:T(8,128)} async-done(((f32[4,256,1024]{2,1,0:T(8,128)}), f32[4,256,1024]{2,1,0:T(8,128)}, u32[]{:S(2)}, u32[]{:S(2)}) %all-to-all-start) | async-done | bytes 4194336 | tf_op jit(solution)/shard_map/all_to_all | solution.py:29
  151.4 59.0 %all-to-all-start.1 = ((s32[64,1,1]{2,1,0:T(1,128)}), s32[64,1,1]{2,1,0:T(1,128)S(1)}, u32[]{:S(2)}, u32[]{:S(2)}) async-start(s32[64,1,1]{2,1,0:T(1,128)} %broadcast_in_dim.141), calls=%async_computation.1 | async-start | bytes 65536 | tf_op jit(solution)/shard_map/all_to_all | solution.py:29
  210.4 3.2 reduce_sum.74
  216.1 3.6 collective-permute-done.5
  219.7 3.2 fusion.35
  226.3 2.3 fusion.38
  229.9 5.0 all-to-all-start.2
  239.3 4.0 copy.113
  243.2 11.5 %all-to-all-done.2 = bf16[4,64,1024]{2,1,0:T(8,128)(2,1)S(1)} async-done(((bf16[4,64,1024]{2,1,0:T(8,128)(2,1)}), bf16[4,64,1024]{2,1,0:T(8,128)(2,1)S(1)}, u32[]{:S(2)}, u32[]{:S(2)}) %all-to-all-start.2) | async-done | bytes 524320 | tf_op jit(solution)/shard_map/all_to_all | solution.py:29
  256.0 5.2 copy.114
  261.2 41.7 %all-gather.29.cloned.1.call-done = bf16[16,4,3,24,512]{4,3,2,1,0:T(8,128)(2,1)} async-done(((bf16[4,4,3,24,512]{4,3,2,1,0:T(8,128)(2,1)}), bf16[16,4,3,24,512]{4,3,2,1,0:T(8,128)(2,1)}) %all-gather.29.cloned.1.call-update) | async-done | bytes 4718608 | tf_op jit(solution)/shard_map/all_gather | solution.py:76
  302.9 6.3 maximum_bitcast_fusion
  311.0 2.2 convolution_bitcast_fusion.1
  316.8 316.5 %all-reduce = s32[4096]{0:T(1024)S(1)} all-reduce(s32[4096]{0:T(1024)S(1)} %select_dynamic-update-slice_fusion), channel_id=1, replica_groups=mesh['seq_0'=4,'seq_1'=4,'seq_2'=4,'tp'=4] {'seq_0','seq_1','seq_2'}, use_global_device_ids=true, to_apply=%add | all-reduce | flops 4096 | bytes 32768
  633.6 2.5 all-gather.17.cloned.1.call-done
  636.1 4.2 slice_bitcast_fusion.1
  644.4 343.3 %all-gather.19.cloned.1.call-done = bf16[512,4096]{0,1:T(8,128)(2,1)} async-done(((bf16[512,64]{0,1:T(8,128)(2,1)}), bf16[512,4096]{0,1:T(8,128)(2,1)}) %all-gather.19.cloned.1.call-update) | async-done | bytes 4194320 | tf_op jit(solution)/shard_map/all_gather | solution.py:323
  987.7 3.7 convolution_bitcast_fusion
  991.4 66.6 %all_to_all.24 = f32[4,64,1024]{2,1,0:T(8,128)S(1)} all-to-all(f32[4,64,1024]{2,1,0:T(8,128)S(1)} %convolution_bitcast_fusion), channel_id=1, replica_groups=mesh['seq_0'=4,'seq_1'=4,'seq_2'=4,'tp'=4] {'tp'}, dimensions={0} | all-to-all | bytes 2097152 | tf_op jit(solution)/shard_map/all_to_all | solution.py:117
  (125 shorter events, 30.7 us)
Async XLA Ops:
  7.2 215.7 %copy-start = (bf16[1024,1024]{1,0:T(8,128)(2,1)S(1)}, bf16[1024,1024]{1,0:T(8,128)(2,1)}, u32[]{:S(2)}) copy-start(bf16[1024,1024]{1,0:T(8,128)(2,1)} %param.17) | copy-start | bytes 6291460
  7.2 56.5 %copy-start.8 = (bf16[1024]{0:T(1024)(128)(2,1)S(1)}, bf16[1024]{0:T(1024)(128)(2,1)}, u32[]{:S(2)}) copy-start(bf16[1024]{0:T(1024)(128)(2,1)} %param.12) | copy-start | bytes 6148
  7.2 56.5 %copy-start.2 = (bf16[256,1024]{1,0:T(8,128)(2,1)S(1)}, bf16[256,1024]{1,0:T(8,128)(2,1)}, u32[]{:S(2)}) copy-start(bf16[256,1024]{1,0:T(8,128)(2,1)} %param.11) | copy-start | bytes 1572868
  7.2 56.4 %all-gather.23.cloned.1.call-start = ((), (), s32[]{:S(2)}) async-start(), calls=%async_computation.7 | async-start | bytes 1474560 | tf_op jit(solution)/shard_map/all_gather | solution.py:76
  20.3 78.8 %all-gather.27.cloned.1.call-start = ((), (), s32[]{:S(2)}) async-start(), calls=%async_computation.9 | async-start | bytes 1474560 | tf_op jit(solution)/shard_map/all_gather | solution.py:76
  31.1 208.2 %all-gather.21.cloned.1.call-start = ((), (), s32[]{:S(2)}) async-start(), calls=%async_computation.6 | async-start | bytes 3932160 | tf_op jit(solution)/shard_map/all_gather | solution.py:76
  58.1 197.9 %all-gather.25.cloned.1.call-start = ((), (), s32[]{:S(2)}) async-start(), calls=%async_computation.8 | async-start | bytes 5898240 | tf_op jit(solution)/shard_map/all_gather | solution.py:76
  66.1 13.7 %collective-permute-start.2 = (bf16[256,256]{0,1:T(8,128)(2,1)S(1)}, bf16[256,256]{0,1:T(8,128)(2,1)S(1)}, u32[]{:S(2)}, u32[]{:S(2)}) collective-permute-start(bf16[256,256]{0,1:T(8,128)(2,1)S(1)} %get-tuple-element.7), channel_id=1, source_target_pairs={{0,8},{4,12},{8,16},{12,20},{16,24},{20,28},{24,32},{28,36},{32,40... | collective-permute-start | bytes 393224 | tf_op jit(solution)/shard_map/ppermute | solution.py:24
  69.6 10.3 collective-permute-start.3
  72.8 9.5 collective-permute-start
  77.0 5.3 collective-permute-start.1
  82.3 1.0 copy-start.5
  86.2 13.5 %copy-start.7 = (s32[1,64]{1,0:T(1,128)S(1)}, s32[1,64]{1,0:T(1,128)}, u32[]{:S(2)}) copy-start(s32[1,64]{1,0:T(1,128)} %param.15) | copy-start | bytes 772
  86.2 15.5 %copy-start.6 = (bf16[4096]{0:T(1024)(128)(2,1)S(1)}, bf16[4096]{0:T(1024)(128)(2,1)}, u32[]{:S(2)}) copy-start(bf16[4096]{0:T(1024)(128)(2,1)} %param.19) | copy-start | bytes 24580
  86.2 64.6 %all-to-all-start = ((f32[4,256,1024]{2,1,0:T(8,128)}), f32[4,256,1024]{2,1,0:T(8,128)}, u32[]{:S(2)}, u32[]{:S(2)}) async-start(f32[4,256,1024]{2,1,0:T(8,128)} %broadcast_in_dim.134), calls=%async_computation | async-start | bytes 8388608 | tf_op jit(solution)/shard_map/all_to_all | solution.py:29
  99.1 203.8 %all-gather.29.cloned.1.call-start = ((), (), s32[]{:S(2)}) async-start(), calls=%async_computation.10 | async-start | bytes 5898240 | tf_op jit(solution)/shard_map/all_gather | solution.py:76
  99.8 4.8 collective-permute-start.4
  151.4 77.6 %all-to-all-start.1 = ((s32[64,1,1]{2,1,0:T(1,128)}), s32[64,1,1]{2,1,0:T(1,128)S(1)}, u32[]{:S(2)}, u32[]{:S(2)}) async-start(s32[64,1,1]{2,1,0:T(1,128)} %broadcast_in_dim.141), calls=%async_computation.1 | async-start | bytes 65536 | tf_op jit(solution)/shard_map/all_to_all | solution.py:29
  214.8 4.9 copy-start.3
  214.8 4.9 collective-permute-start.5
  222.9 3.4 copy-start.4
  229.9 24.8 %all-to-all-start.2 = ((bf16[4,64,1024]{2,1,0:T(8,128)(2,1)}), bf16[4,64,1024]{2,1,0:T(8,128)(2,1)S(1)}, u32[]{:S(2)}, u32[]{:S(2)}) async-start(bf16[4,64,1024]{2,1,0:T(8,128)(2,1)} %broadcast_in_dim.145), calls=%async_computation.2 | async-start | bytes 1048576 | tf_op jit(solution)/shard_map/all_to_all | solution.py:29
  234.9 401.2 %all-gather.17.cloned.1.call-start = ((), (), s32[]{:S(2)}) async-start(), calls=%async_computation.4 | async-start | bytes 8519680 | tf_op jit(solution)/shard_map/all_gather | solution.py:99
  311.0 4.3 copy-start.9
  314.5 673.1 %all-gather.19.cloned.1.call-start = ((), (), s32[]{:S(2)}) async-start(), calls=%async_computation.5 | async-start | bytes 4259840 | tf_op jit(solution)/shard_map/all_gather | solution.py:323
  987.7 71.2 %copy-start.1 = (bf16[1024,1024]{1,0:T(8,128)(2,1)S(1)}, bf16[1024,1024]{1,0:T(8,128)(2,1)}, u32[]{:S(2)}) copy-start(bf16[1024,1024]{1,0:T(8,128)(2,1)} %param.17) | copy-start | bytes 6291460
Sparse Core Ops, SparseCore 0:
  20.4 43.1 all-gather.22
  65.4 24.5 all-gather.26
  91.8 47.5 all-gather.20
  141.1 55.4 all-gather.24
  198.2 104.6 all-gather.28
  314.7 321.3 all-gather.16
  637.9 349.7 all-gather.18
where the time goes:
time: 1070 us
  waiting for transfers between devices  457 us (43%)
  blocking collectives  432 us (40%)
  starting transfers between devices  93.1 us (9%)
  local copies, waits for them, and re-layouts  25.2 us (2%)
  matrix products  22 us (2%)
  other arithmetic  18.3 us (2%)
  between operations  17.9 us (2%)
    all_gather x1, waiting for transfers between devices, shards(): lax.all_gather(lat_proj_out, SEQ, axis=1, tiled=True)  343 us
    unnamed x1, blocking collectives  317 us
    all_to_all x3, starting transfers between devices, from_everyone(): return lax.all_to_all(copies, axis, split_axis=0, concat_axis=0, tiled=True)  76.9 us
    all_to_all x1, blocking collectives, sum_at_owner(): lax.all_to_all(in_blocks(value, dim, length), axis, 0, 0, tiled=True)  66.6 us
    all_to_all x3, waiting for transfers between devices, from_everyone(): return lax.all_to_all(copies, axis, split_axis=0, concat_axis=0, tiled=True)  56.7 us
    all_gather x4, blocking collectives, gather_in_order(): tiles = lax.all_gather(tiles, axes[k])  48.8 us
    all_gather x5, waiting for transfers between devices, gather_in_order(): tiles = lax.all_gather(tiles, axes[k])  47.2 us
  transfers between devices with their start and end apart: 16, of which 8 were waited for; matrix products, arithmetic and copies ran while one was open for 5% of the time, Pallas kernels for 0%

commit v1 on v0

v1 whole, which is shorter than its diff:
```python
import math

import jax
import jax.numpy as jnp
from jax import lax
from jax.sharding import Mesh
from jax.sharding import PartitionSpec as P

EH = 64
HD = 128
WIN = 512
SPILL = 8
ZL, RX, RY, ZH, CO = ("z_lo", "ring_x", "ring_y", "z_hi", "core")
SEQ = (ZL, RX, RY)
TP = (ZH, CO)
ROWS = (RX, RY)
COLUMN = (ZL, ZH, CO)

epsilon = 1e-05
rope_base = 500000.0
far_position = 1 << 30
bf16 = jnp.bfloat16
f32 = jnp.float32


def shifted(value, axis, steps):
    count = lax.axis_size(axis)
    leading, last = (max(0, -steps), min(count, count - steps))
    return lax.ppermute(value, axis, [(source, source + steps) for source in range(leading, last)])


def exchanged(pieces, axis):
    return lax.all_to_all(pieces, axis, split_axis=0, concat_axis=0, tiled=True)


def gathered(value, axis):
    return exchanged(jnp.broadcast_to(value, (lax.axis_size(axis), *value.shape)), axis)


def rms_factor(values):
    return lax.rsqrt(jnp.mean(values * values, axis=-1, keepdims=True) + epsilon)


def masked_softmax(scores, allowed):
    scores = jnp.where(allowed, scores, -1e30)
    largest = jnp.max(scores, axis=-1, keepdims=True)
    raised = jnp.where(allowed, jnp.exp(scores - largest), 0.0)
    return raised / jnp.sum(raised, axis=-1, keepdims=True)


def rotate(values, position):
    halfway = values.shape[-1] // 2
    frequency = jnp.power(rope_base, -2.0 * jnp.arange(halfway, dtype=f32) / values.shape[-1])
    angles = position.astype(f32)[:, None] * frequency[None, :]
    cosine, sine = (jnp.cos(angles), jnp.sin(angles))
    lower, upper = (values[..., :halfway], values[..., halfway:])
    return jnp.concatenate(
        [lower * cosine - upper * sine, upper * cosine + lower * sine], axis=-1
    )


def encoder_heads(normed, weights):
    return jnp.einsum("bd,idc->ibc", normed, weights, preferred_element_type=f32).astype(bf16)


def encoder_attention(queries, keys_values, anchor):
    rows, width = queries.shape
    heads = width // EH
    spans = keys_values.shape[0]
    keys, values = (keys_values[:, :width], keys_values[:, width:])
    scores = jnp.einsum(
        "qhd,khd->hqk",
        queries.reshape(rows, heads, EH),
        keys.reshape(spans, heads, EH),
        preferred_element_type=f32,
    ) * (1.0 / math.sqrt(EH))
    query_pos = anchor + jnp.arange(rows, dtype=jnp.int32)
    key_pos = anchor - WIN + jnp.arange(spans, dtype=jnp.int32)
    allowed = (
        (key_pos[None, :] <= query_pos[:, None])
        & (key_pos[None, :] > query_pos[:, None] - WIN)
        & (key_pos[None, :] >= 0)
    )
    weights = masked_softmax(scores, allowed[None]).astype(bf16)
    attended = jnp.einsum(
        "hqk,khd->qhd", weights, values.reshape(spans, heads, EH), preferred_element_type=f32
    )
    return attended.reshape(rows, width).astype(bf16)


def patch_block(extended, first_byte, end_byte, in_use, anchor, lift, cross_kv):
    columns = anchor + jnp.arange(extended.shape[0], dtype=jnp.int32)
    inside = (
        (columns[None, :] >= first_byte[:, None])
        & (columns[None, :] < end_byte[:, None])
        & in_use[:, None]
    )
    member = inside.astype(bf16)
    totals = jnp.dot(member, extended, preferred_element_type=f32)
    lengths = jnp.maximum(jnp.sum(inside.astype(f32), axis=1), 1.0)
    pooled = (totals / lengths[:, None]).astype(bf16)
    lifted = jnp.dot(pooled, lift, preferred_element_type=f32)
    key_rows = jnp.dot(extended, cross_kv[0], preferred_element_type=f32).astype(bf16)
    value_rows = jnp.dot(extended, cross_kv[1], preferred_element_type=f32).astype(bf16)
    slot_total = first_byte.shape[0]
    head_count = lifted.shape[1] // HD
    queries = lifted.astype(bf16).reshape(slot_total, head_count, HD)
    scores = jnp.einsum(
        "phd,khd->hpk",
        queries,
        key_rows.reshape(-1, head_count, HD),
        preferred_element_type=f32,
    ) * (1.0 / math.sqrt(HD))
    allowed = inside | (~in_use)[:, None] & (columns[None, :] == anchor)
    weights = masked_softmax(scores, allowed[None]).astype(bf16)
    crossed = jnp.einsum(
        "hpk,khd->phd",
        weights,
        value_rows.reshape(-1, head_count, HD),
        preferred_element_type=f32,
    )
    crossed = crossed.reshape(slot_total, head_count * HD)
    return jnp.where(in_use[:, None], lifted + crossed, 0.0).astype(bf16)


def shards(
    byte_states,
    enc_gain,
    enc_qkv,
    enc_proj_out,
    starts,
    counts,
    lift,
    cross_kv,
    latent_gain,
    lat_qkv,
    lat_proj_out,
):
    byte_rows, byte_width = byte_states.shape
    slots = starts.shape[1]
    columns = lax.axis_size(ZL)
    tensor = lax.axis_size(TP)
    groups = lax.axis_size(ROWS)
    anchor = lax.axis_index(SEQ) * byte_rows
    local_starts = starts[0]
    patch_count = counts[0]
    slot_ids = jnp.arange(slots, dtype=jnp.int32)
    in_use = slot_ids < patch_count

    first_local = (local_starts[0] - anchor).astype(bf16)
    edge = jnp.concatenate(
        [byte_states[:SPILL], jnp.broadcast_to(first_local, (SPILL, byte_width))], axis=0
    )
    edge = shifted(edge, SEQ, -1)
    next_first = edge[SPILL, 0].astype(jnp.int32)

    gain = enc_gain.astype(f32)
    states = byte_states.astype(f32)
    own = encoder_heads((states * rms_factor(states) * gain).astype(bf16), enc_qkv)
    own_kv = jnp.concatenate([own[1], own[2]], axis=1)
    far_kv = shifted(own_kv, SEQ, 2)
    near_kv = shifted(own_kv, SEQ, 1)

    share, depth, inner = lat_qkv.shape
    by_head = lat_qkv.reshape(share * depth, columns, HD).transpose(1, 0, 2)
    mark = jnp.broadcast_to(counts.astype(bf16), (columns, 16, HD))
    by_head = exchanged(jnp.concatenate([by_head, mark], axis=1), ZL)
    by_head = gathered(by_head, ROWS)
    all_counts = by_head[:, :, share * depth, 0].astype(jnp.int32).T
    latent_in = by_head[:, :, : share * depth].reshape(groups, columns, share, depth, HD)
    latent_in = latent_in.transpose(1, 0, 3, 2, 4).reshape(-1, share * HD)
    latent_in = (latent_in.astype(f32) * latent_gain.astype(f32)[:, None]).astype(bf16)

    enc_out = gathered(gathered(enc_proj_out, ZH), CO)

    out_part = gathered(lat_proj_out.T, TP)
    turned = [
        (a * tensor + b, b * tensor + a) for a in range(columns) for b in range(tensor)
    ]
    out_part = lax.ppermute(out_part, COLUMN, turned)
    out_part = gathered(out_part, ROWS)

    extra = edge[:SPILL].astype(f32)
    more = encoder_heads((extra * rms_factor(extra) * gain).astype(bf16), enc_qkv)
    more_kv = jnp.concatenate([more[1], more[2]], axis=1)
    queries = jnp.concatenate([own[0], more[0]], axis=0)
    keys_values = jnp.concatenate([far_kv, near_kv, own_kv, more_kv], axis=0)
    attended = gathered(encoder_attention(queries, keys_values, anchor), TP)
    attended = attended.reshape(*(lax.axis_size(name) for name in TP), *attended.shape[1:])
    blended = jnp.einsum("zcbw,czwd->bd", attended, enc_out, preferred_element_type=f32)
    extended = (jnp.concatenate([states, extra], axis=0) + blended).astype(bf16)
    encoded = extended[:byte_rows]

    following = jnp.concatenate([local_starts[1:], jnp.zeros((1,), jnp.int32)])
    patch_end = jnp.where(slot_ids + 1 < patch_count, following, anchor + byte_rows + next_first)
    patches = patch_block(extended, local_starts, patch_end, in_use, anchor, lift, cross_kv)

    rows = gathered(gathered(patches, (ZL, ZH)), CO)
    rows = rows.reshape(2, columns, 2, slots, -1).transpose(1, 3, 2, 0, 4)
    rows = rows.reshape(columns * slots, -1)
    factor = rms_factor(rows.astype(f32))
    projected = jnp.dot(rows, latent_in, preferred_element_type=f32) * factor

    flat_counts = all_counts.reshape(-1)
    block_ids = jnp.arange(flat_counts.shape[0], dtype=jnp.int32)
    offsets = jnp.sum(
        jnp.where(block_ids[None, :] < block_ids[:, None], flat_counts[None, :], 0), axis=1
    ).reshape(columns, groups)
    own_offsets = lax.dynamic_slice_in_dim(offsets, lax.axis_index(ROWS), 1, axis=1)
    position = (own_offsets + slot_ids[None, :]).reshape(-1)
    key_pos = jnp.where(
        slot_ids < all_counts.T[:, :, None], offsets.T[:, :, None] + slot_ids, far_position
    ).reshape(-1)
    queries = rotate(projected[:, :HD], position).astype(bf16)
    keys = rotate(projected[:, HD : 2 * HD], position).astype(bf16)
    keys_values = jnp.concatenate([keys, projected[:, 2 * HD :].astype(bf16)], axis=1)
    keys_values = gathered(keys_values, ROWS).reshape(-1, 2 * HD)
    scores = jnp.dot(
        queries, keys_values[:, :HD].T, preferred_element_type=f32
    ) * (1.0 / math.sqrt(HD))
    allowed = key_pos[None, :] <= position[:, None]
    scores = jnp.where(allowed, scores, -1e30)
    largest = jnp.max(scores, axis=-1, keepdims=True)
    raised = jnp.where(allowed, jnp.exp(scores - largest), 0.0)
    weighted = jnp.dot(raised.astype(bf16), keys_values[:, HD:], preferred_element_type=f32)
    heads = (weighted / jnp.sum(raised, axis=-1, keepdims=True)).astype(bf16)

    heads = jnp.broadcast_to(
        heads.reshape(columns, 1, slots, HD), (columns, tensor, slots, HD)
    ).reshape(columns * tensor, slots, HD)
    heads = exchanged(heads, COLUMN).reshape(columns, tensor, slots, HD)
    heads = heads.transpose(2, 1, 0, 3).reshape(slots, tensor, columns * HD)
    reduced = jnp.einsum("ptk,gtjk->pgj", heads, out_part, preferred_element_type=f32)
    reduced = reduced.reshape(slots, -1)
    latent = jnp.where(in_use[:, None], patches.astype(f32) + reduced, 0.0).astype(bf16)
    return (encoded, latent)


def solution(mesh):
    finer = Mesh(mesh.devices.reshape(4, 4, 4, 2, 2), (*SEQ, *TP))
    in_specs = (
        P(SEQ, None),
        P(),
        P(None, None, TP),
        P(TP, None),
        P(SEQ, None),
        P(SEQ),
        P(None, TP),
        P(None, None, TP),
        P(),
        P(None, SEQ, TP),
        P(TP, SEQ),
    )
    out_specs = (P(SEQ, None), P(SEQ, TP))
    return jax.shard_map(
        shards, mesh=finer, in_specs=in_specs, out_specs=out_specs, check_vma=False
    )
```

time: 1070 us -> 341 us (0.32)
  blocking collectives: 432 us -> 48.8 us
  waiting for transfers between devices: 457 us -> 118 us
  between operations: 17.9 us -> 2.42 us
  local copies, waits for them, and re-layouts: 25.2 us -> 39.2 us
    all_gather x7 -> x0, waiting for transfers between devices: 393 us -> none  [the longest x1 343 us: shards(): lax.all_gather(lat_proj_out, SEQ, axis=1, tiled=True)]
    unnamed x1 -> x0, blocking collectives: 317 us -> none
    all_to_all x3 -> x8, waiting for transfers between devices: 56.7 us -> 114 us  [exchanged(): return lax.all_to_all(pieces, axis, split_axis=0, concat_axis=0, tiled=True)]
    all_gather x4 -> x0, blocking collectives: 48.8 us -> none  [gather_in_order(): tiles = lax.all_gather(tiles, axes[k])]
    all_to_all x1 -> x3, blocking collectives: 66.6 us -> 48.8 us  [exchanged(): return lax.all_to_all(pieces, axis, split_axis=0, concat_axis=0, tiled=True)]
    all_to_all x3 -> x8, starting transfers between devices: 76.9 us -> 71.1 us  [exchanged(): return lax.all_to_all(pieces, axis, split_axis=0, concat_axis=0, tiled=True)]
  transfers between devices with their start and end apart: 16 -> 12, of which waited for: 8 -> 6; matrix products, arithmetic and copies ran while one was open for 5% -> 18% of each run, Pallas kernels for 0% -> 0%
where the time goes in v1:
time: 341 us; the launch traced here: 339 us
  waiting for transfers between devices  118 us (35%)
  starting transfers between devices  87.9 us (26%)
  blocking collectives  48.8 us (14%)
  local copies, waits for them, and re-layouts  39.2 us (11%)
  matrix products  29.6 us (9%)
  other arithmetic  13 us (4%)
    all_to_all x8, waiting for transfers between devices, exchanged(): return lax.all_to_all(pieces, axis, split_axis=0, concat_axis=0, tiled=True)  114 us
    all_to_all x8, starting transfers between devices, exchanged(): return lax.all_to_all(pieces, axis, split_axis=0, concat_axis=0, tiled=True)  71.1 us
    all_to_all x3, blocking collectives, exchanged(): return lax.all_to_all(pieces, axis, split_axis=0, concat_axis=0, tiled=True)  48.8 us
    ppermute x3, starting transfers between devices, shifted(): lax.ppermute(value, axis, [(source, source + steps) for source in range(l...  10.6 us
    broadcast_in_dim x9, local copies, waits for them, and re-layouts, gathered(): jnp.broadcast_to(value, (lax.axis_size(axis), *value.shape))  9.78 us
  transfers between devices with their start and end apart: 12, of which 6 were waited for; matrix products, arithmetic and copies ran while one was open for 18% of the time, Pallas kernels for 0%

profile of v1, /device:TPU:1, one launch (start us, length us, event | category | flops | bytes accessed | tf_op | source)
XLA Modules:
  0.0 339.2 jit_solution(14805006571401774766)
XLA Ops:
  2.8 2.4 fusion.39
  6.5 4.7 %collective-permute-start.2 = (bf16[256,512]{0,1:T(8,128)(2,1)}, bf16[256,512]{0,1:T(8,128)(2,1)}, u32[]{:S(2)}, u32[]{:S(2)}) collective-permute-start(bf16[256,512]{0,1:T(8,128)(2,1)} %pad_maximum_fusion.1), channel_id=1, source_target_pairs={{0,4},{4,8},{8,12},{12,16},{16,20},{20,24},{24,28},{28,32},{32,36}... | collective-permute-start | bytes 786440 | tf_op jit(solution)/shard_map/ppermute | solution.py:29
  11.3 4.6 %collective-permute-start.1 = (bf16[256,512]{0,1:T(8,128)(2,1)}, bf16[256,512]{0,1:T(8,128)(2,1)}, u32[]{:S(2)}, u32[]{:S(2)}) collective-permute-start(bf16[256,512]{0,1:T(8,128)(2,1)} %pad_maximum_fusion.1), channel_id=1, source_target_pairs={{0,8},{4,12},{8,16},{12,20},{16,24},{20,28},{24,32},{28,36},{32,40... | collective-permute-start | bytes 786440 | tf_op jit(solution)/shard_map/ppermute | solution.py:29
  19.1 8.2 %all-to-all-start.1 = ((bf16[2,256,1024]{2,1,0:T(8,128)(2,1)}), bf16[2,256,1024]{2,1,0:T(8,128)(2,1)S(1)}, u32[]{:S(2)}, u32[]{:S(2)}) async-start(bf16[2,256,1024]{2,1,0:T(8,128)(2,1)} %broadcast_in_dim.162), calls=%async_computation.1 | async-start | bytes 2097152 | tf_op jit(solution)/shard_map/all_to_all | solution.py:33
  42.3 5.0 %fusion.131 = (f32[4,264]{1,0:T(4,128)S(1)}, f32[4,264,776]{2,1,0:T(8,128)}) fusion(pred[264,776]{1,0:T(8,128)(4,1)} %and_and_fusion, bf16[776,4,64]{0,2,1:T(8,128)(2,1)} %bitcast.168, bf16[8,4,64]{0,2,1:T(8,128)(2,1)} %bitcast.173, bf16[256,4,64]{0,2,1:T(8,128)(2,1)} %bitcast.170), kind=kOutput, calls=%fused_computation.159 | convolution fusion | flops 109258760 | bytes 4019392 | tf_op jit(solution)/shard_map/sub | solution.py:47
  47.3 3.1 fusion.43
  50.8 12.4 %all_to_all.55 = bf16[2,2,256,1024]{3,2,1,0:T(8,128)(2,1)} all-to-all(bf16[2,2,256,1024]{3,2,1,0:T(8,128)(2,1)S(1)} %broadcast_in_dim.163), channel_id=1, replica_groups=mesh['z_lo'=4,'ring_x'=4,'ring_y'=4,'z_hi'=2,'core'=2] {'core'}, dimensions={0} | all-to-all | bytes 4194304 | tf_op jit(solution)/shard_map/all_to_all | solution.py:33
  64.1 3.8 %all-to-all-start = ((bf16[4,264,256]{2,1,0:T(8,128)(2,1)}), bf16[4,264,256]{2,1,0:T(8,128)(2,1)S(1)}, u32[]{:S(2)}, u32[]{:S(2)}) async-start(bf16[4,264,256]{2,1,0:T(8,128)(2,1)} %broadcast_in_dim.161), calls=%async_computation | async-start | bytes 1081344 | tf_op jit(solution)/shard_map/all_to_all | solution.py:33
  68.3 11.7 %all-to-all-done = bf16[4,264,256]{2,1,0:T(8,128)(2,1)S(1)} async-done(((bf16[4,264,256]{2,1,0:T(8,128)(2,1)}), bf16[4,264,256]{2,1,0:T(8,128)(2,1)S(1)}, u32[]{:S(2)}, u32[]{:S(2)}) %all-to-all-start) | async-done | bytes 540704 | tf_op jit(solution)/shard_map/all_to_all | solution.py:33
  80.1 11.7 %all-to-all-start.3 = ((bf16[4,208,128]{2,1,0:T(8,128)(2,1)}), bf16[4,208,128]{2,1,0:T(8,128)(2,1)S(1)}, u32[]{:S(2)}, u32[]{:S(2)}) async-start(bf16[4,208,128]{2,1,0:T(8,128)(2,1)} %concatenate.55.clone), calls=%async_computation.3 | async-start | bytes 425984 | tf_op jit(solution)/shard_map/all_to_all | solution.py:33
  91.8 2.9 fusion.56
  102.1 27.0 %all_to_all.56 = bf16[8,64,1024]{2,1,0:T(8,128)(2,1)S(1)} all-to-all(bf16[8,64,1024]{2,1,0:T(8,128)(2,1)S(1)} %broadcast_in_dim.175), channel_id=1, replica_groups=mesh['z_lo'=4,'ring_x'=4,'ring_y'=4,'z_hi'=2,'core'=2] {'z_lo','z_hi'}, dimensions={0} | all-to-all | bytes 2097152 | tf_op jit(solution)/shard_map/all_to_all | solution.py:33
  129.3 9.4 %all_to_all.57 = bf16[2,8,64,1024]{3,2,1,0:T(8,128)(2,1)S(1)} all-to-all(bf16[2,8,64,1024]{3,2,1,0:T(8,128)(2,1)S(1)} %broadcast_in_dim.176), channel_id=1, replica_groups=mesh['z_lo'=4,'ring_x'=4,'ring_y'=4,'z_hi'=2,'core'=2] {'core'}, dimensions={0} | all-to-all | bytes 4194304 | tf_op jit(solution)/shard_map/all_to_all | solution.py:33
  138.7 2.4 broadcast_in_dim.170
  141.1 4.8 %all-to-all-start.4 = ((bf16[16,4,208,128]{3,2,1,0:T(8,128)(2,1)}), bf16[16,4,208,128]{3,2,1,0:T(8,128)(2,1)}, u32[]{:S(2)}, u32[]{:S(2)}) async-start(bf16[16,4,208,128]{3,2,1,0:T(8,128)(2,1)} %broadcast_in_dim.170), calls=%async_computation.4 | async-start | bytes 6815744 | tf_op jit(solution)/shard_map/all_to_all | solution.py:33
  146.1 3.5 %copy.139 = bf16[4,64,2,2,1024]{4,3,2,1,0:T(2,128)(2,1)} copy(bf16[4,64,2,2,1024]{4,1,2,0,3:T(8,128)(2,1)S(1)} %bitcast.157) | data formatting | bytes 4194304 | tf_op jit(solution)/shard_map/transpose | solution.py:199
  149.6 4.5 %reshape.418 = bf16[256,4096]{1,0:T(8,128)(2,1)} reshape(bf16[4,64,2,2,1024]{4,3,2,1,0:T(2,128)(2,1)} %copy.139) | data formatting | bytes 4194304 | tf_op jit(solution)/shard_map/reshape | solution.py:200
  154.8 38.2 %all-to-all-done.4 = bf16[16,4,208,128]{3,2,1,0:T(8,128)(2,1)} async-done(((bf16[16,4,208,128]{3,2,1,0:T(8,128)(2,1)}), bf16[16,4,208,128]{3,2,1,0:T(8,128)(2,1)}, u32[]{:S(2)}, u32[]{:S(2)}) %all-to-all-start.4) | async-done | bytes 3407904 | tf_op jit(solution)/shard_map/all_to_all | solution.py:33
  193.7 5.0 %all-to-all-start.9 = ((bf16[4,64,512]{2,1,0:T(8,128)(2,1)}), bf16[4,64,512]{2,1,0:T(8,128)(2,1)S(1)}, u32[]{:S(2)}, u32[]{:S(2)}) async-start(bf16[4,64,512]{2,1,0:T(8,128)(2,1)} %broadcast_in_dim.182), calls=%async_computation.9 | async-start | bytes 524288 | tf_op jit(solution)/shard_map/all_to_all | solution.py:33
  200.1 2.2 slice.122
  203.6 3.1 copy.141
  210.4 11.8 %all-to-all-start.7 = ((bf16[16,256,256]{2,1,0:T(8,128)(2,1)}), bf16[16,256,256]{2,1,0:T(8,128)(2,1)S(1)}, u32[]{:S(2)}, u32[]{:S(2)}) async-start(bf16[16,256,256]{2,1,0:T(8,128)(2,1)} %broadcast_in_dim.177), calls=%async_computation.7 | async-start | bytes 4194304 | tf_op jit(solution)/shard_map/all_to_all | solution.py:33
  222.2 6.3 %collective-permute-start.3 = (bf16[4,64,512]{2,1,0:T(8,128)(2,1)S(1)}, bf16[4,64,512]{2,1,0:T(8,128)(2,1)S(1)}, u32[]{:S(2)}, u32[]{:S(2)}) collective-permute-start(bf16[4,64,512]{2,1,0:T(8,128)(2,1)S(1)} %all-to-all-done.9), channel_id=1, source_target_pairs={{0,0},{1,64},{2,128},{3,192},{64,1},{65,65},{66,129},{67,193},{128... | collective-permute-start | bytes 786440 | tf_op jit(solution)/shard_map/ppermute | solution.py:180
  228.5 4.3 %collective-permute-done.3 = bf16[4,64,512]{2,1,0:T(8,128)(2,1)S(1)} collective-permute-done((bf16[4,64,512]{2,1,0:T(8,128)(2,1)S(1)}, bf16[4,64,512]{2,1,0:T(8,128)(2,1)S(1)}, u32[]{:S(2)}, u32[]{:S(2)}) %collective-permute-start.3) | collective-permute-done | bytes 262176 | tf_op jit(solution)/shard_map/ppermute | solution.py:180
  232.9 14.7 %all-to-all-done.7 = bf16[16,256,256]{2,1,0:T(8,128)(2,1)S(1)} async-done(((bf16[16,256,256]{2,1,0:T(8,128)(2,1)}), bf16[16,256,256]{2,1,0:T(8,128)(2,1)S(1)}, u32[]{:S(2)}, u32[]{:S(2)}) %all-to-all-start.7) | async-done | bytes 2097184 | tf_op jit(solution)/shard_map/all_to_all | solution.py:33
  247.6 2.5 broadcast_in_dim.183
  250.0 6.5 %all-to-all-start.10 = ((bf16[16,4,64,512]{3,2,1,0:T(8,128)(2,1)}), bf16[16,4,64,512]{3,2,1,0:T(8,128)(2,1)}, u32[]{:S(2)}, u32[]{:S(2)}) async-start(bf16[16,4,64,512]{3,2,1,0:T(8,128)(2,1)} %broadcast_in_dim.183), calls=%async_computation.10 | async-start | bytes 8388608 | tf_op jit(solution)/shard_map/all_to_all | solution.py:33
  260.2 43.1 %all-to-all-done.10 = bf16[16,4,64,512]{3,2,1,0:T(8,128)(2,1)} async-done(((bf16[16,4,64,512]{3,2,1,0:T(8,128)(2,1)}), bf16[16,4,64,512]{3,2,1,0:T(8,128)(2,1)}, u32[]{:S(2)}, u32[]{:S(2)}) %all-to-all-start.10) | async-done | bytes 4194336 | tf_op jit(solution)/shard_map/all_to_all | solution.py:33
  304.0 19.2 %all-to-all-start.8 = ((bf16[16,64,128]{2,1,0:T(8,128)(2,1)}), bf16[16,64,128]{2,1,0:T(8,128)(2,1)S(1)}, u32[]{:S(2)}, u32[]{:S(2)}) async-start(bf16[16,64,128]{2,1,0:T(8,128)(2,1)} %bitcast.38), calls=%async_computation.8 | async-start | bytes 524288 | tf_op jit(solution)/shard_map/all_to_all | solution.py:33
  324.1 4.8 %copy.145 = bf16[16,64,512,4]{2,1,0,3:T(8,128)(2,1)} copy(bf16[16,64,512,4]{2,1,3,0:T(8,128)(2,1)} %bitcast.42) | data formatting | bytes 8388608 | tf_op jit(solution)/shard_map/ptk,gtjk->pgj/dot_general | solution.py:233
  328.9 6.1 %all-to-all-done.8 = bf16[16,64,128]{2,1,0:T(8,128)(2,1)S(1)} async-done(((bf16[16,64,128]{2,1,0:T(8,128)(2,1)}), bf16[16,64,128]{2,1,0:T(8,128)(2,1)S(1)}, u32[]{:S(2)}, u32[]{:S(2)}) %all-to-all-start.8) | async-done | bytes 262176 | tf_op jit(solution)/shard_map/all_to_all | solution.py:33
  335.0 4.2 %fusion.47 = bf16[64,1024]{1,0:T(8,128)(2,1)} fusion(bf16[1024,512,4]{1,0,2:T(8,128)(2,1)} %bitcast.159, bf16[4,4,8,8,128]{4,3,2,1,0:T(8,128)(2,1)S(1)} %bitcast.164, bf16[64,1024]{1,0:T(8,128)(2,1)S(1)} %fusion.77, pred[64]{0:T(512)(128)(4,1)S(1)} %iota_compare_fusion.2), kind=kOutput, calls=%fused_computation.49 | convolution fusion | flops 268697600 | bytes 4718656 | tf_op jit(solution)/shard_map/ptk,gtjk->pgj/dot_general | solution.py:233
  (118 shorter events, 42.5 us)
Async XLA Ops:
  0.6 97.6 %copy-start = (bf16[1024,1024]{1,0:T(8,128)(2,1)S(1)}, bf16[1024,1024]{1,0:T(8,128)(2,1)}, u32[]{:S(2)}) copy-start(bf16[1024,1024]{1,0:T(8,128)(2,1)} %param.17) | copy-start | bytes 6291460
  0.6 15.2 %copy-start.13 = (pred[16]{0:T(512)(128)(4,1)S(1)}, pred[16]{0:T(512)(128)(4,1)}, u32[]{:S(2)}) copy-start(pred[16]{0:T(512)(128)(4,1)} %constant.24.clone.1) | copy-start | bytes 52
  0.7 15.2 %copy-start.9 = (s32[1,64]{1,0:T(1,128)S(1)}, s32[1,64]{1,0:T(1,128)}, u32[]{:S(2)}) copy-start(s32[1,64]{1,0:T(1,128)} %param.15) | copy-start | bytes 772
  0.7 17.3 %copy-start.4 = (bf16[256,1024]{1,0:T(8,128)(2,1)S(1)}, bf16[256,1024]{1,0:T(8,128)(2,1)}, u32[]{:S(2)}) copy-start(bf16[256,1024]{1,0:T(8,128)(2,1)} %param.14) | copy-start | bytes 1572868
  6.5 33.7 %collective-permute-start.2 = (bf16[256,512]{0,1:T(8,128)(2,1)}, bf16[256,512]{0,1:T(8,128)(2,1)}, u32[]{:S(2)}, u32[]{:S(2)}) collective-permute-start(bf16[256,512]{0,1:T(8,128)(2,1)} %pad_maximum_fusion.1), channel_id=1, source_target_pairs={{0,4},{4,8},{8,12},{12,16},{16,20},{20,24},{24,28},{28,32},{32,36}... | collective-permute-start | bytes 786440 | tf_op jit(solution)/shard_map/ppermute | solution.py:29
  11.3 29.0 %collective-permute-start.1 = (bf16[256,512]{0,1:T(8,128)(2,1)}, bf16[256,512]{0,1:T(8,128)(2,1)}, u32[]{:S(2)}, u32[]{:S(2)}) collective-permute-start(bf16[256,512]{0,1:T(8,128)(2,1)} %pad_maximum_fusion.1), channel_id=1, source_target_pairs={{0,8},{4,12},{8,16},{12,20},{16,24},{20,28},{24,32},{28,36},{32,40... | collective-permute-start | bytes 786440 | tf_op jit(solution)/shard_map/ppermute | solution.py:29
  16.7 19.5 %collective-permute-start = (bf16[16,1024]{1,0:T(8,128)(2,1)S(1)}, bf16[16,1024]{1,0:T(8,128)(2,1)S(1)}, u32[]{:S(2)}, u32[]{:S(2)}) collective-permute-start(bf16[16,1024]{1,0:T(8,128)(2,1)S(1)} %slice_select_fusion), channel_id=1, source_target_pairs={{4,0},{8,4},{12,8},{16,12},{20,16},{24,20},{28,24},{32,28},{36,32}... | collective-permute-start | bytes 98312 | tf_op jit(solution)/shard_map/ppermute | solution.py:29
  19.1 31.4 %all-to-all-start.1 = ((bf16[2,256,1024]{2,1,0:T(8,128)(2,1)}), bf16[2,256,1024]{2,1,0:T(8,128)(2,1)S(1)}, u32[]{:S(2)}, u32[]{:S(2)}) async-start(bf16[2,256,1024]{2,1,0:T(8,128)(2,1)} %broadcast_in_dim.162), calls=%async_computation.1 | async-start | bytes 2097152 | tf_op jit(solution)/shard_map/all_to_all | solution.py:33
  36.2 3.8 %copy-start.5 = (bf16[16,1024]{1,0:T(8,128)(2,1)}, bf16[16,1024]{1,0:T(8,128)(2,1)S(1)}, u32[]{:S(2)}) copy-start(bf16[16,1024]{1,0:T(8,128)(2,1)S(1)} %collective-permute-done) | copy-start | bytes 98308
  50.8 17.2 %copy-start.14 = (s32[63]{0:T(128)S(1)}, s32[63]{0:T(128)}, u32[]{:S(2)}) copy-start(s32[63]{0:T(128)} %slice_bitcast_fusion.4) | copy-start | bytes 760
  50.8 17.2 %copy-start.10 = (s32[1,64]{1,0:T(1,128)S(1)}, s32[1,64]{1,0:T(1,128)}, u32[]{:S(2)}) copy-start(s32[1,64]{1,0:T(1,128)} %param.15) | copy-start | bytes 772
  50.8 17.4 %copy-start.11 = (pred[264]{0:T(512)(128)(4,1)S(1)}, pred[264]{0:T(512)(128)(4,1)}, u32[]{:S(2)}) copy-start(pred[264]{0:T(512)(128)(4,1)} %fusion.109) | copy-start | bytes 796
  50.8 17.4 %copy-start.12 = (pred[64]{0:T(512)(128)(4,1)S(1)}, pred[64]{0:T(512)(128)(4,1)}, u32[]{:S(2)}) copy-start(pred[64]{0:T(512)(128)(4,1)} %fusion.127) | copy-start | bytes 196
  50.8 17.5 %copy-start.6 = (bf16[16,1024]{1,0:T(8,128)(2,1)S(1)}, bf16[16,1024]{1,0:T(8,128)(2,1)}, u32[]{:S(2)}) copy-start(bf16[16,1024]{1,0:T(8,128)(2,1)} %copy-done.5) | copy-start | bytes 98308
  64.1 16.0 %all-to-all-start = ((bf16[4,264,256]{2,1,0:T(8,128)(2,1)}), bf16[4,264,256]{2,1,0:T(8,128)(2,1)S(1)}, u32[]{:S(2)}, u32[]{:S(2)}) async-start(bf16[4,264,256]{2,1,0:T(8,128)(2,1)} %broadcast_in_dim.161), calls=%async_computation | async-start | bytes 1081344 | tf_op jit(solution)/shard_map/all_to_all | solution.py:33
  80.1 11.7 %copy-start.3 = (bf16[4,264,256]{2,1,0:T(8,128)(2,1)}, bf16[4,264,256]{2,1,0:T(8,128)(2,1)S(1)}, u32[]{:S(2)}) copy-start(bf16[4,264,256]{2,1,0:T(8,128)(2,1)S(1)} %all-to-all-done) | copy-start | bytes 1622020
  80.1 21.9 %all-to-all-start.3 = ((bf16[4,208,128]{2,1,0:T(8,128)(2,1)}), bf16[4,208,128]{2,1,0:T(8,128)(2,1)S(1)}, u32[]{:S(2)}, u32[]{:S(2)}) async-start(bf16[4,208,128]{2,1,0:T(8,128)(2,1)} %concatenate.55.clone), calls=%async_computation.3 | async-start | bytes 425984 | tf_op jit(solution)/shard_map/all_to_all | solution.py:33
  91.8 3.3 copy-start.15
  141.1 4.8 %copy-start.8 = (bf16[4096]{0:T(1024)(128)(2,1)S(1)}, bf16[4096]{0:T(1024)(128)(2,1)}, u32[]{:S(2)}) copy-start(bf16[4096]{0:T(1024)(128)(2,1)} %param.19) | copy-start | bytes 24580
  141.1 51.8 %all-to-all-start.4 = ((bf16[16,4,208,128]{3,2,1,0:T(8,128)(2,1)}), bf16[16,4,208,128]{3,2,1,0:T(8,128)(2,1)}, u32[]{:S(2)}, u32[]{:S(2)}) async-start(bf16[16,4,208,128]{3,2,1,0:T(8,128)(2,1)} %broadcast_in_dim.170), calls=%async_computation.4 | async-start | bytes 6815744 | tf_op jit(solution)/shard_map/all_to_all | solution.py:33
  149.6 43.4 %copy-start.7 = (bf16[512,64]{0,1:T(8,128)(2,1)S(1)}, bf16[512,64]{0,1:T(8,128)(2,1)}, u32[]{:S(2)}) copy-start(bf16[512,64]{0,1:T(8,128)(2,1)} %param.21) | copy-start | bytes 196612
  193.7 15.1 %all-to-all-start.9 = ((bf16[4,64,512]{2,1,0:T(8,128)(2,1)}), bf16[4,64,512]{2,1,0:T(8,128)(2,1)S(1)}, u32[]{:S(2)}, u32[]{:S(2)}) async-start(bf16[4,64,512]{2,1,0:T(8,128)(2,1)} %broadcast_in_dim.182), calls=%async_computation.9 | async-start | bytes 524288 | tf_op jit(solution)/shard_map/all_to_all | solution.py:33
  203.5 3.3 copy-start.2
  210.4 37.1 %all-to-all-start.7 = ((bf16[16,256,256]{2,1,0:T(8,128)(2,1)}), bf16[16,256,256]{2,1,0:T(8,128)(2,1)S(1)}, u32[]{:S(2)}, u32[]{:S(2)}) async-start(bf16[16,256,256]{2,1,0:T(8,128)(2,1)} %broadcast_in_dim.177), calls=%async_computation.7 | async-start | bytes 4194304 | tf_op jit(solution)/shard_map/all_to_all | solution.py:33
  222.2 10.6 %collective-permute-start.3 = (bf16[4,64,512]{2,1,0:T(8,128)(2,1)S(1)}, bf16[4,64,512]{2,1,0:T(8,128)(2,1)S(1)}, u32[]{:S(2)}, u32[]{:S(2)}) collective-permute-start(bf16[4,64,512]{2,1,0:T(8,128)(2,1)S(1)} %all-to-all-done.9), channel_id=1, source_target_pairs={{0,0},{1,64},{2,128},{3,192},{64,1},{65,65},{66,129},{67,193},{128... | collective-permute-start | bytes 786440 | tf_op jit(solution)/shard_map/ppermute | solution.py:180
  250.0 53.2 %all-to-all-start.10 = ((bf16[16,4,64,512]{3,2,1,0:T(8,128)(2,1)}), bf16[16,4,64,512]{3,2,1,0:T(8,128)(2,1)}, u32[]{:S(2)}, u32[]{:S(2)}) async-start(bf16[16,4,64,512]{3,2,1,0:T(8,128)(2,1)} %broadcast_in_dim.183), calls=%async_computation.10 | async-start | bytes 8388608 | tf_op jit(solution)/shard_map/all_to_all | solution.py:33
  304.0 30.9 %all-to-all-start.8 = ((bf16[16,64,128]{2,1,0:T(8,128)(2,1)}), bf16[16,64,128]{2,1,0:T(8,128)(2,1)S(1)}, u32[]{:S(2)}, u32[]{:S(2)}) async-start(bf16[16,64,128]{2,1,0:T(8,128)(2,1)} %bitcast.38), calls=%async_computation.8 | async-start | bytes 524288 | tf_op jit(solution)/shard_map/all_to_all | solution.py:33
  324.1 15.1 %copy-start.1 = (bf16[1024,1024]{1,0:T(8,128)(2,1)S(1)}, bf16[1024,1024]{1,0:T(8,128)(2,1)}, u32[]{:S(2)}) copy-start(bf16[1024,1024]{1,0:T(8,128)(2,1)} %param.17) | copy-start | bytes 6291460
